TPU v7x, 512 devices: a whole 4x4x16 slice. The times are simulated.
512 devices in a mesh: head: 16 (over y, x), tok: 32 (over z, core).
Axes of the slice: x: 4, y: 4, z: 16, core: 2. Of those that a mesh axis runs over, the one named last changes fastest.
Arguments:
- stretch_tokens: bfloat16 [32, 1024, 1792], P('tok', 'head'), may hold values from -6 to 6
- stretch_tail: bfloat16 [32, 2, 1792], P('tok'), may hold values from -6 to 6
- decode_tokens: bfloat16 [32, 32, 1792], P('tok'), may hold values from -6 to 6
- decode_tail: bfloat16 [32, 32, 2, 1792], P('tok'), may hold values from -6 to 6
- norm_gain: float32 [1792], replicated, may hold values from 0.1 to 1.9
- conv_taps: float32 [3, 1792], replicated, may hold values from -3 to 3
- qkv_weight: bfloat16 [1792, 16, 144], P(None, 'head'), may hold values from -0.125 to 0.125
- out_gain: float32 [1792], P('head'), may hold values from 0.1 to 1.9
- out_weight: bfloat16 [1792, 1792], P('head'), may hold values from -0.125 to 0.125
- state_cache: float32 [32, 16, 16, 112, 273], P('tok', None, 'head'), may hold values from -24 to 24
- stretch_len: int32 [32], P('tok'), may hold values from 1 to 1024, 16384 in all
- stretch_slot: int32 [32], P('tok'), may hold values from 0 to 15
- decode_slot: int32 [32, 32], P('tok'), may hold values from 0 to 15
- decode_owner: int32 [32, 32, 1], P('tok'), may hold values from 0 to 31; in each aligned block of 32 rows (0 to 31, 32 to 63, ..., all dimensions but the last counted through in order) at most 2 rows name the same one
Outputs:
- stretch_out: bfloat16 [32, 1024, 1792], P('tok', 'head')
- decode_out: bfloat16 [32, 32, 1792], P('tok', 'head')
- state_new: float32 [32, 16, 112, 273], P('tok', 'head')
Inputs may be any that keep to these rules, and one draw needn't show every extreme that they name: `decode_owner`: in the 32 decoders of one group at most 2 name the same owner group, a bound that some block reaches of them. `stretch_len`: some group's stretch is full.
All inputs are finite; a program needn't handle non-finite values.
Results may differ from a plain program's by a relative error of at most 0.014.
Values may be sent and summed in bfloat16 or wider, within the bound.
A program may use at most 64 MiB of HBM per device.

v0:
```python
import math
import jax
import jax.numpy as jnp
from jax import lax
from jax.sharding import PartitionSpec as P

D = 1792
DH = 112
F = 16
STRETCH = 1024
DEC = 32


def from_behind(array, axis, by):
    peers = lax.axis_size(axis)
    pairs = [(i, i + by) for i in range(peers) if 0 <= i + by < peers]
    return lax.ppermute(array, axis, pairs)


def rms_rows(values, gain):
    values = values.astype(jnp.float32)
    factor = lax.rsqrt(jnp.mean(values * values, axis=-1, keepdims=True) + 1e-05)
    return values * factor * gain


def features(vectors):
    breadth = vectors.shape[-1]
    linear = vectors / math.sqrt(math.sqrt(breadth))
    outer = vectors[..., :, None] * vectors[..., None, :] / math.sqrt(2.0 * breadth)
    outer = outer.reshape(vectors.shape[:-1] + (breadth * breadth,))
    ones = jnp.ones(vectors.shape[:-1] + (1,), vectors.dtype)
    return jnp.concatenate([ones, linear, outer], axis=-1)


def convolve(tail, normed, conv_taps):
    joined = jnp.concatenate([tail, normed], axis=-2).astype(jnp.float32)
    span_rows = normed.shape[-2]
    total = conv_taps[0] * joined[..., 0:span_rows, :]
    total = total + conv_taps[1] * joined[..., 1 : span_rows + 1, :]
    total = total + conv_taps[2] * joined[..., 2 : span_rows + 2, :]
    return total.astype(jnp.bfloat16)


def decode_items(items, slot_items, cache_own, out_gain, head_count):
    item_count = items.shape[0]
    shaped = items.reshape(item_count, head_count, 2 * F + DH).astype(jnp.float32)
    queries = shaped[:, :, :F]
    key_feats = shaped[:, :, F : 2 * F]
    values = shaped[:, :, 2 * F :]
    slot_total = cache_own.shape[0]
    table = jnp.einsum(
        "nhp,shdp->nshd", features(queries), cache_own, precision=lax.Precision.HIGHEST
    )
    picker = (slot_items[:, None] == jnp.arange(slot_total)[None, :]).astype(jnp.float32)
    carried = jnp.einsum("ns,nshd->nhd", picker, table, precision=lax.Precision.HIGHEST)
    inner = jnp.sum(queries * key_feats, axis=-1) / math.sqrt(F)
    own_term = (1.0 + inner + 0.5 * inner * inner)[..., None] * values
    attended = rms_rows(carried + own_term, out_gain.reshape(head_count, DH))
    return attended.astype(jnp.bfloat16).reshape(item_count, head_count * DH)


def local(
    stretch_tokens,
    stretch_tail,
    decode_tokens,
    decode_tail,
    norm_gain,
    conv_taps,
    qkv_weight,
    out_gain,
    out_weight,
    state_cache,
    stretch_len,
    stretch_slot,
    decode_slot,
    decode_owner,
):
    head_count = qkv_weight.shape[1]
    block_width = qkv_weight.shape[2]
    rows_own = stretch_tokens.shape[1]
    w_flat = qkv_weight.reshape(D, head_count * block_width)
    gains = out_gain.reshape(head_count, DH)
    normed = rms_rows(stretch_tokens[0], norm_gain).astype(jnp.bfloat16)
    rim_rows = from_behind(normed[rows_own - 2 :], "head", 1)
    first_dev = lax.axis_index("head") == 0
    rim_rows = jnp.where(first_dev, stretch_tail[0], rim_rows)
    conved = convolve(rim_rows, normed, conv_taps)
    grouped = jnp.dot(
        lax.all_gather(conved, "head", axis=0, tiled=True),
        w_flat,
        preferred_element_type=jnp.float32,
    ).astype(jnp.bfloat16)
    grouped = grouped.reshape(STRETCH, head_count, block_width)
    queries = grouped[:, :, :F]
    key_feats = grouped[:, :, F : 2 * F]
    values = grouped[:, :, 2 * F :]
    length = stretch_len[0]
    positions = jnp.arange(STRETCH)
    valid_rows = positions < length
    state_old = lax.dynamic_index_in_dim(state_cache[0], stretch_slot[0], 0, keepdims=False)
    carried = jnp.einsum(
        "ihp,hdp->ihd",
        features(queries.astype(jnp.float32)),
        state_old,
        precision=lax.Precision.HIGHEST,
    )
    block_rows = min(512, STRETCH)
    pieces = []
    for anchor in range(0, STRETCH, block_rows):
        finish = anchor + block_rows
        inner = jnp.einsum(
            "ihf,jhf->hij",
            queries[anchor:finish],
            key_feats[:finish],
            preferred_element_type=jnp.float32,
        ) / math.sqrt(F)
        weights = 1.0 + inner + 0.5 * inner * inner
        allowed = (positions[None, :finish] <= positions[anchor:finish, None]) & valid_rows[
            None, :finish
        ]
        weights = jnp.where(allowed[None], weights, 0.0).astype(jnp.bfloat16)
        pieces.append(
            jnp.einsum("hij,jhd->ihd", weights, values[:finish], preferred_element_type=jnp.float32)
        )
    local_sum = jnp.concatenate(pieces, axis=0)
    attended = rms_rows(carried + local_sum, gains)
    attended = (
        jnp.where(valid_rows[:, None, None], attended, 0.0)
        .astype(jnp.bfloat16)
        .reshape(STRETCH, head_count * DH)
    )
    key_phi = jnp.where(
        valid_rows[:, None, None], features(key_feats.astype(jnp.float32)), 0.0
    ).astype(jnp.bfloat16)
    state_next = state_old + jnp.einsum(
        "jhd,jhp->hdp", values, key_phi, preferred_element_type=jnp.float32
    )
    stretch_part = jnp.dot(attended, out_weight, preferred_element_type=jnp.float32).astype(
        jnp.bfloat16
    )
    dec_normed = rms_rows(decode_tokens[0], norm_gain).astype(jnp.bfloat16)
    dec_conved = convolve(decode_tail[0], dec_normed[:, None, :], conv_taps)[:, 0, :]
    dec_qkv = jnp.dot(dec_conved, w_flat, preferred_element_type=jnp.float32).astype(jnp.bfloat16)
    owners = decode_owner[0, :, 0]
    slots_here = decode_slot[0]
    groups = lax.axis_size("tok")
    capacity = max(2, 2 * DEC // groups)
    earlier = jnp.arange(DEC)[None, :] < jnp.arange(DEC)[:, None]
    same_owner = owners[None, :] == owners[:, None]
    rank_in = jnp.sum(earlier & same_owner, axis=1)
    target = owners * capacity + rank_in
    placing = jnp.arange(groups * capacity)[:, None] == target[None, :]
    sent_rows = jnp.dot(
        placing.astype(jnp.bfloat16), dec_qkv, preferred_element_type=jnp.float32
    ).astype(jnp.bfloat16)
    sent_rows = sent_rows.reshape(groups, capacity, head_count * block_width)
    sent_slots = jnp.sum(jnp.where(placing, slots_here[None, :] + 1, 0), axis=1) - 1
    sent_slots = sent_slots.reshape(groups, capacity, 1).astype(jnp.bfloat16)
    sent_rows = jnp.concatenate([sent_rows, sent_slots], axis=2)
    item_rows = lax.all_to_all(sent_rows, "tok", split_axis=0, concat_axis=0, tiled=True)
    item_slots = item_rows[:, :, -1].astype(jnp.int32)
    item_rows = item_rows[:, :, :-1]
    item_count = item_rows.shape[1]
    flat_out = decode_items(
        item_rows.reshape(groups * item_count, head_count * block_width),
        item_slots.reshape(groups * item_count),
        state_cache[0],
        out_gain,
        head_count,
    )
    served = flat_out.reshape(groups, item_count, head_count * DH)
    returned = lax.all_to_all(served, "tok", split_axis=0, concat_axis=0, tiled=True)
    dec_attended = jnp.dot(
        jnp.transpose(placing).astype(jnp.bfloat16),
        returned.reshape(groups * capacity, head_count * DH),
        preferred_element_type=jnp.float32,
    ).astype(jnp.bfloat16)
    dec_part = jnp.dot(dec_attended, out_weight, preferred_element_type=jnp.float32).astype(
        jnp.bfloat16
    )
    heads = lax.axis_size("head")
    pad_rows = 16
    dec_part = dec_part.reshape(heads, DEC // heads, D)
    dec_part = jnp.pad(dec_part, ((0, 0), (0, pad_rows - DEC // heads), (0, 0)))
    both = jnp.concatenate([stretch_part.reshape(heads, rows_own, D), dec_part], axis=1)
    summed = lax.psum_scatter(
        both.reshape(heads * (rows_own + pad_rows), D), "head", scatter_dimension=0, tiled=True
    )
    stretch_out = summed[:rows_own]
    decode_out = summed[rows_own : rows_own + DEC // heads]
    return (stretch_out[None], decode_out[None], state_next[None])


def solution(mesh):
    in_specs = (
        P("tok", "head", None),
        P("tok", None, None),
        P("tok", None, None),
        P("tok", None, None, None),
        P(),
        P(),
        P(None, "head", None),
        P("head"),
        P("head", None),
        P("tok", None, "head", None, None),
        P("tok"),
        P("tok"),
        P("tok", None),
        P("tok", None, None),
    )
    out_specs = (P("tok", "head", None), P("tok", "head", None), P("tok", "head", None, None))
    return jax.shard_map(local, mesh=mesh, in_specs=in_specs, out_specs=out_specs, check_vma=False)
```

profile of v0, /device:TPU:2, one launch (start us, length us, event | category | flops | bytes accessed | tf_op | source)
XLA Modules:
  0.0 199.8 jit_solution(16442440949846528474)
XLA Ops:
  7.3 1.2 fusion.39
  8.5 1.1 fusion.41
  9.6 3.4 %collective-permute-start = (bf16[2,1792]{1,0:T(2,128)(2,1)S(1)}, bf16[2,1792]{1,0:T(2,128)(2,1)S(1)}, u32[]{:S(2)}, u32[]{:S(2)}) collective-permute-start(bf16[2,1792]{1,0:T(2,128)(2,1)S(1)} %slice.116), channel_id=1, source_target_pairs={{0,32},{32,64},{64,96},{96,128},{128,160},{160,192},{192,224},{224... | collective-permute-start | bytes 21512 | tf_op jit(solution)/shard_map/ppermute | solution.py:17
  13.0 0.9 slice_reduce_fusion.2
  14.0 4.4 %collective-permute-done = bf16[2,1792]{1,0:T(2,128)(2,1)S(1)} collective-permute-done((bf16[2,1792]{1,0:T(2,128)(2,1)S(1)}, bf16[2,1792]{1,0:T(2,128)(2,1)S(1)}, u32[]{:S(2)}, u32[]{:S(2)}) %collective-permute-start) | collective-permute-done | bytes 7200 | tf_op jit(solution)/shard_map/ppermute | solution.py:17
  18.4 0.7 broadcast_select_fusion
  19.2 0.8 fusion.43
  21.4 0.7 pad_maximum_fusion
  22.1 12.2 %all-to-all-start = ((bf16[32,2,145]{2,1,0:T(2,128)(2,1)}), bf16[32,2,145]{2,1,0:T(2,128)(2,1)S(1)}, u32[]{:S(2)}, u32[]{:S(2)}) async-start(bf16[32,2,145]{2,1,0:T(2,128)(2,1)} %pad_maximum_fusion), calls=%async_computation | async-start | bytes 65536 | tf_op jit(solution)/shard_map/all_to_all | solution.py:160
  35.7 11.6 %all-to-all-done = bf16[32,2,145]{2,1,0:T(2,128)(2,1)S(1)} async-done(((bf16[32,2,145]{2,1,0:T(2,128)(2,1)}), bf16[32,2,145]{2,1,0:T(2,128)(2,1)S(1)}, u32[]{:S(2)}, u32[]{:S(2)}) %all-to-all-start) | async-done | bytes 18592 | tf_op jit(solution)/shard_map/all_to_all | solution.py:160
  48.5 0.7 copy.42
  49.3 2.6 %fusion.2 = f32[64,16,112]{2,0,1:T(8,128)S(1)} fusion(f32[1,16,1,112,273]{3,2,4,1,0:T(1,128)S(1)} %copy-done.1, f32[64,1,256]{2,0,1:T(8,128)} %copy.42, f32[64,1,16]{2,0,1:T(8,128)S(1)} %get-tuple-element.20, f32[273]{0:T(512)S(1)} %pad.10.clone), kind=kOutput, calls=%fused_computation.4 | convolution fusion | flops 375752832 | bytes 2486340 | tf_op jit(solution)/shard_map/nhp,shdp->nshd/dot_general | solution.py:51
  53.5 3.8 %all-to-all-start.1 = ((bf16[32,2,112]{2,1,0:T(2,128)(2,1)}), bf16[32,2,112]{2,1,0:T(2,128)(2,1)S(1)}, u32[]{:S(2)}, u32[]{:S(2)}) async-start(bf16[32,2,112]{2,1,0:T(2,128)(2,1)} %bitcast.39), calls=%async_computation.1 | async-start | bytes 32768 | tf_op jit(solution)/shard_map/all_to_all | solution.py:172
  57.5 12.3 %all-to-all-done.1 = bf16[32,2,112]{2,1,0:T(2,128)(2,1)S(1)} async-done(((bf16[32,2,112]{2,1,0:T(2,128)(2,1)}), bf16[32,2,112]{2,1,0:T(2,128)(2,1)S(1)}, u32[]{:S(2)}, u32[]{:S(2)}) %all-to-all-start.1) | async-done | bytes 14368 | tf_op jit(solution)/shard_map/all_to_all | solution.py:172
  70.1 15.6 %all-gather.2.cloned.1.call-done = bf16[1024,1792]{1,0:T(8,128)(2,1)} async-done(((bf16[64,1792]{1,0:T(8,128)(2,1)}), bf16[1024,1792]{1,0:T(8,128)(2,1)}) %all-gather.2.cloned.1.call-update) | async-done | bytes 3670032 | tf_op jit(solution)/shard_map/all_gather | solution.py:89
  85.7 3.4 %fusion.8 = bf16[1024,1,144]{0,2,1:T(8,128)(2,1)S(1)} fusion(bf16[1024,1792]{1,0:T(8,128)(2,1)} %all-gather.2.cloned.1.call-done, bf16[1792,1,144]{0,2,1:T(8,128)(2,1)S(1)} %copy-done), kind=kOutput, calls=%fused_computation.15 | convolution fusion | flops 528629760 | bytes 4481024 | tf_op jit(solution)/shard_map/dot_general | solution.py:88
  89.1 1.1 fusion.9
  91.0 1.2 multiply_reduce_fusion
  92.2 1.2 convolution_convert_fusion
  93.5 2.4 %fusion.1 = bf16[16,80,1792]{2,1,0:T(8,128)(2,1)} fusion(bf16[16,2,1792]{2,1,0:T(2,128)(2,1)S(1)} %reshape.515, bf16[16,64,1792]{2,1,0:T(8,128)(2,1)S(1)} %bitcast.135), kind=kLoop, calls=%fused_computation.2 | loop fusion | flops 13762560 | bytes 8372224 | tf_op jit(solution)/shard_map/concatenate | solution.py:185
  96.5 0.8 copy.45
  97.3 92.7 %reduce-scatter.2.cloned.1.call-done = bf16[80,1792]{1,0:T(8,128)(2,1)} async-done(((bf16[1280,1792]{1,0:T(8,128)(2,1)}), bf16[80,1792]{1,0:T(8,128)(2,1)}) %reduce-scatter.2.cloned.1.call-update) | async-done | bytes 286736 | tf_op jit(solution)/shard_map/reduce_scatter | solution.py:186
  190.0 1.3 slice_bitcast_fusion.16
  191.4 1.6 slice_bitcast_fusion
  (71 shorter events, 6.1 us)
Async XLA Ops:
  7.2 13.7 %copy-start = (bf16[1792,1,144]{0,2,1:T(8,128)(2,1)S(1)}, bf16[1792,1,144]{0,2,1:T(8,128)(2,1)}, u32[]{:S(2)}) copy-start(bf16[1792,1,144]{0,2,1:T(8,128)(2,1)} %param.20) | copy-start | bytes 1548292
  7.2 13.5 %copy-start.5 = (f32[1792]{0:T(1024)S(1)}, f32[1792]{0:T(1024)}, u32[]{:S(2)}) copy-start(f32[1792]{0:T(1024)} %param.18) | copy-start | bytes 21508
  7.2 12.9 %copy-start.9 = (s32[1,32,1]{1,2,0:T(1,128)S(1)}, s32[1,32,1]{1,2,0:T(1,128)}, u32[]{:S(2)}) copy-start(s32[1,32,1]{1,2,0:T(1,128)} %param.27) | copy-start | bytes 388
  7.2 13.0 %copy-start.8 = (s32[1,32]{1,0:T(1,128)S(1)}, s32[1,32]{1,0:T(1,128)}, u32[]{:S(2)}) copy-start(s32[1,32]{1,0:T(1,128)} %param.26) | copy-start | bytes 388
  7.2 13.3 %copy-start.4 = (bf16[1,32,2,1792]{3,2,1,0:T(2,128)(2,1)S(1)}, bf16[1,32,2,1792]{3,2,1,0:T(2,128)(2,1)}, u32[]{:S(2)}) copy-start(bf16[1,32,2,1792]{3,2,1,0:T(2,128)(2,1)} %param.17) | copy-start | bytes 688132
  7.2 13.3 %copy-start.3 = (bf16[1,32,1792]{2,1,0:T(8,128)(2,1)S(1)}, bf16[1,32,1792]{2,1,0:T(8,128)(2,1)}, u32[]{:S(2)}) copy-start(bf16[1,32,1792]{2,1,0:T(8,128)(2,1)} %param.16) | copy-start | bytes 344068
  7.2 78.5 %all-gather.2.cloned.1.call-start = ((), (), s32[]{:S(2)}) async-start(), calls=%async_computation.3 | async-start | bytes 3899392 | tf_op jit(solution)/shard_map/all_gather | solution.py:89
  9.6 8.8 %collective-permute-start = (bf16[2,1792]{1,0:T(2,128)(2,1)S(1)}, bf16[2,1792]{1,0:T(2,128)(2,1)S(1)}, u32[]{:S(2)}, u32[]{:S(2)}) collective-permute-start(bf16[2,1792]{1,0:T(2,128)(2,1)S(1)} %slice.116), channel_id=1, source_target_pairs={{0,32},{32,64},{64,96},{96,128},{128,160},{160,192},{192,224},{224... | collective-permute-start | bytes 21512 | tf_op jit(solution)/shard_map/ppermute | solution.py:17
  19.2 16.5 %copy-start.1 = (f32[1,16,1,112,273]{3,2,4,1,0:T(1,128)S(1)}, f32[1,16,1,112,273]{3,2,4,1,0:T(1,128)}, u32[]{:S(2)}) copy-start(f32[1,16,1,112,273]{3,2,4,1,0:T(1,128)} %param.23) | copy-start | bytes 5870596
  22.1 25.2 %all-to-all-start = ((bf16[32,2,145]{2,1,0:T(2,128)(2,1)}), bf16[32,2,145]{2,1,0:T(2,128)(2,1)S(1)}, u32[]{:S(2)}, u32[]{:S(2)}) async-start(bf16[32,2,145]{2,1,0:T(2,128)(2,1)} %pad_maximum_fusion), calls=%async_computation | async-start | bytes 65536 | tf_op jit(solution)/shard_map/all_to_all | solution.py:160
  35.7 17.1 %copy-start.7 = (f32[112]{0:T(128)S(1)}, f32[112]{0:T(128)}, u32[]{:S(2)}) copy-start(f32[112]{0:T(128)} %param.21) | copy-start | bytes 1348
  48.1 21.6 %copy-start.2 = (bf16[112,1792]{1,0:T(8,128)(2,1)S(1)}, bf16[112,1792]{1,0:T(8,128)(2,1)}, u32[]{:S(2)}) copy-start(bf16[112,1792]{1,0:T(8,128)(2,1)} %param.22) | copy-start | bytes 1204228
  53.5 16.2 %all-to-all-start.1 = ((bf16[32,2,112]{2,1,0:T(2,128)(2,1)}), bf16[32,2,112]{2,1,0:T(2,128)(2,1)S(1)}, u32[]{:S(2)}, u32[]{:S(2)}) async-start(bf16[32,2,112]{2,1,0:T(2,128)(2,1)} %bitcast.39), calls=%async_computation.1 | async-start | bytes 32768 | tf_op jit(solution)/shard_map/all_to_all | solution.py:172
  57.3 132.7 %reduce-scatter.2.cloned.1.call-start = ((), (), s32[]{:S(2)}) async-start(), calls=%async_computation.4 | async-start | bytes 4874240 | tf_op jit(solution)/shard_map/reduce_scatter | solution.py:186
  57.4 31.6 %copy-start.6 = (s32[1024]{0:T(1024)}, s32[1024]{0:T(1024)S(1)}, u32[]{:S(2)}) copy-start(s32[1024]{0:T(1024)S(1)} %iota.31) | copy-start | bytes 12292
  89.1 1.2 slice-start
Sparse Core Ops, SparseCore 0:
  20.2 65.4 all-gather.1
  96.0 93.9 reduce-scatter.1
where the time goes:
time: 200 us
  waiting for transfers between devices  137 us (68%)
  starting transfers between devices  19.6 us (10%)
  between operations  15.8 us (8%)
  matrix products  12.1 us (6%)
  other arithmetic  9.75 us (5%)
  local copies, waits for them, and re-layouts  6 us (3%)
    reduce_scatter x1, waiting for transfers between devices, local(): lax.psum_scatter(both.reshape(heads * (rows_own + pad_rows), D), 'head',...  92.7 us
    all_gather x1, waiting for transfers between devices, local(): lax.all_gather(conved, 'head', axis=0, tiled=True)  15.6 us
    all_to_all x1, waiting for transfers between devices, local(): lax.all_to_all(served, 'tok', split_axis=0, concat_axis=0, tiled=True)  12.3 us
    all_to_all x1, starting transfers between devices, local(): lax.all_to_all(sent_rows, 'tok', split_axis=0, concat_axis=0, tiled=True)  12.2 us
    all_to_all x1, waiting for transfers between devices, local(): lax.all_to_all(sent_rows, 'tok', split_axis=0, concat_axis=0, tiled=True)  11.6 us
    ppermute x1, waiting for transfers between devices, from_behind(): return lax.ppermute(array, axis, pairs)  4.44 us
  transfers between devices with their start and end apart: 5, of which 5 were waited for; matrix products, arithmetic and copies ran while one was open for 5% of the time, Pallas kernels for 0%

commit v1 on v0

--- a/solution.py
+++ b/solution.py
@@ -1,3 +1,4 @@
+import functools
 import math
 import jax
 import jax.numpy as jnp
@@ -9,6 +10,14 @@
 F = 16
 STRETCH = 1024
 DEC = 32
+
+
+def _unite_packet(vector, on_dim):
+    met_up = jnp.concatenate([vector for _ in range(lax.psum(1, "head"))], axis=on_dim)
+    return lax.all_to_all(met_up, "head", on_dim, on_dim, tiled=True)
+
+
+_search_bench = functools.partial(_unite_packet, on_dim=0)
 
 
 def from_behind(array, axis, by):
@@ -85,11 +94,9 @@
     first_dev = lax.axis_index("head") == 0
     rim_rows = jnp.where(first_dev, stretch_tail[0], rim_rows)
     conved = convolve(rim_rows, normed, conv_taps)
-    grouped = jnp.dot(
-        lax.all_gather(conved, "head", axis=0, tiled=True),
-        w_flat,
-        preferred_element_type=jnp.float32,
-    ).astype(jnp.bfloat16)
+    grouped = jnp.dot(_search_bench(conved), w_flat, preferred_element_type=jnp.float32).astype(
+        jnp.bfloat16
+    )
     grouped = grouped.reshape(STRETCH, head_count, block_width)
     queries = grouped[:, :, :F]
     key_feats = grouped[:, :, F : 2 * F]

time: 200 us -> 243 us (1.22)
  starting transfers between devices: 19.6 us -> 36.3 us
  local copies, waits for them, and re-layouts: 6 us -> 17.7 us
  waiting for transfers between devices: 137 us -> 148 us
  other arithmetic: 9.75 us -> 12.8 us
    all_to_all x0 -> x1, waiting for transfers between devices: none -> 48.8 us  [_unite_packet(): return lax.all_to_all(met_up, 'head', on_dim, on_dim, tiled=True)]
    all_gather x1 -> x0, waiting for transfers between devices: 15.6 us -> none  [local(): lax.all_gather(conved, 'head', axis=0, tiled=True)]
    unnamed x22 -> x30, local copies, waits for them, and re-layouts: 0.89 us -> 12.5 us
    all_to_all x1, waiting for transfers between devices: 11.6 us -> 2.09 us  [local(): lax.all_to_all(sent_rows, 'tok', split_axis=0, concat_axis=0, tiled=True)]
    reduce_scatter x1, waiting for transfers between devices: 92.7 us -> 85.3 us  [local(): lax.psum_scatter(both.reshape(heads * (rows_own + pad_rows), D), 'head',...]
    all_to_all x0 -> x1, starting transfers between devices: none -> 7.31 us  [_unite_packet(): return lax.all_to_all(met_up, 'head', on_dim, on_dim, tiled=True)]
    all_to_all x1, starting transfers between devices: 3.83 us -> 10.1 us  [local(): lax.all_to_all(served, 'tok', split_axis=0, concat_axis=0, tiled=True)]
    ppermute x1, waiting for transfers between devices: 4.44 us -> 0.01 us  [from_behind(): return lax.ppermute(array, axis, pairs)]
  transfers between devices with their start and end apart: 5 -> 5, of which waited for: 5 -> 4; matrix products, arithmetic and copies ran while one was open for 5% -> 9% of each run, Pallas kernels for 0% -> 0%
where the time goes in v1:
time: 243 us; the launch traced here: 242 us
  waiting for transfers between devices  148 us (61%)
  starting transfers between devices  36.3 us (15%)
  local copies, waits for them, and re-layouts  17.7 us (7%)
  between operations  15.8 us (7%)
  other arithmetic  12.8 us (5%)
  matrix products  11.3 us (5%)
    reduce_scatter x1, waiting for transfers between devices, local(): lax.psum_scatter(both.reshape(heads * (rows_own + pad_rows), D), 'head',...  85.3 us
    all_to_all x1, waiting for transfers between devices, _unite_packet(): return lax.all_to_all(met_up, 'head', on_dim, on_dim, tiled=True)  48.8 us
    all_to_all x1, starting transfers between devices, local(): lax.all_to_all(sent_rows, 'tok', split_axis=0, concat_axis=0, tiled=True)  15.5 us
    unnamed x30, local copies, waits for them, and re-layouts  12.5 us
    all_to_all x1, waiting for transfers between devices, local(): lax.all_to_all(served, 'tok', split_axis=0, concat_axis=0, tiled=True)  11.7 us
    all_to_all x1, starting transfers between devices, local(): lax.all_to_all(served, 'tok', split_axis=0, concat_axis=0, tiled=True)  10.1 us
    all_to_all x1, starting transfers between devices, _unite_packet(): return lax.all_to_all(met_up, 'head', on_dim, on_dim, tiled=True)  7.31 us
  transfers between devices with their start and end apart: 5, of which 4 were waited for; matrix products, arithmetic and copies ran while one was open for 9% of the time, Pallas kernels for 0%

profile of v1, /device:TPU:2, one launch (start us, length us, event | category | flops | bytes accessed | tf_op | source)
XLA Modules:
  0.0 241.9 jit_solution(7615202542930090720)
XLA Ops:
  7.2 1.1 fusion.39
  8.3 1.1 fusion.41
  9.4 3.4 %collective-permute-start = (bf16[2,1792]{1,0:T(2,128)(2,1)S(1)}, bf16[2,1792]{1,0:T(2,128)(2,1)S(1)}, u32[]{:S(2)}, u32[]{:S(2)}) collective-permute-start(bf16[2,1792]{1,0:T(2,128)(2,1)S(1)} %slice.116), channel_id=1, source_target_pairs={{0,32},{32,64},{64,96},{96,128},{128,160},{160,192},{192,224},{224... | collective-permute-start | bytes 21512 | tf_op jit(solution)/shard_map/ppermute | solution.py:26
  13.5 0.9 convert_reduce_fusion.1
  15.2 1.0 fusion.48
  16.4 0.9 slice_reduce_fusion.2
  17.3 1.0 fusion.47
  18.3 1.0 copy.67
  20.5 15.5 %all-to-all-start.1 = ((bf16[32,2,145]{2,1,0:T(2,128)(2,1)}), bf16[32,2,145]{2,1,0:T(2,128)(2,1)S(1)}, u32[]{:S(2)}, u32[]{:S(2)}) async-start(bf16[32,2,145]{2,1,0:T(2,128)(2,1)} %pad_maximum_fusion), calls=%async_computation.1 | async-start | bytes 65536 | tf_op jit(solution)/shard_map/all_to_all | solution.py:167
  36.2 0.8 constant_dynamic-update-slice_fusion.15
  46.9 2.1 all-to-all-done.1
  50.4 1.8 fusion.2
  53.8 10.1 %all-to-all-start.2 = ((bf16[32,2,112]{2,1,0:T(2,128)(2,1)}), bf16[32,2,112]{2,1,0:T(2,128)(2,1)S(1)}, u32[]{:S(2)}, u32[]{:S(2)}) async-start(bf16[32,2,112]{2,1,0:T(2,128)(2,1)} %bitcast.41), calls=%async_computation.2 | async-start | bytes 32768 | tf_op jit(solution)/shard_map/all_to_all | solution.py:179
  64.6 11.7 %all-to-all-done.2 = bf16[32,2,112]{2,1,0:T(2,128)(2,1)S(1)} async-done(((bf16[32,2,112]{2,1,0:T(2,128)(2,1)}), bf16[32,2,112]{2,1,0:T(2,128)(2,1)S(1)}, u32[]{:S(2)}, u32[]{:S(2)}) %all-to-all-start.2) | async-done | bytes 14368 | tf_op jit(solution)/shard_map/all_to_all | solution.py:179
  76.3 7.3 %all-to-all-start = ((bf16[16,64,1792]{2,1,0:T(8,128)(2,1)}), bf16[16,64,1792]{2,1,0:T(8,128)(2,1)}, u32[]{:S(2)}, u32[]{:S(2)}) async-start(bf16[16,64,1792]{2,1,0:T(8,128)(2,1)} %bitcast.5), calls=%async_computation | async-start | bytes 7340032 | tf_op jit(solution)/shard_map/all_to_all | solution.py:17
  85.5 48.8 %all-to-all-done = bf16[16,64,1792]{2,1,0:T(8,128)(2,1)} async-done(((bf16[16,64,1792]{2,1,0:T(8,128)(2,1)}), bf16[16,64,1792]{2,1,0:T(8,128)(2,1)}, u32[]{:S(2)}, u32[]{:S(2)}) %all-to-all-start) | async-done | bytes 3670048 | tf_op jit(solution)/shard_map/all_to_all | solution.py:17
  134.3 3.4 %fusion.8 = bf16[1024,1,144]{0,2,1:T(8,128)(2,1)S(1)} fusion(bf16[1024,1792]{1,0:T(8,128)(2,1)} %bitcast.6, bf16[1792,1,144]{0,2,1:T(8,128)(2,1)S(1)} %copy-done), kind=kOutput, calls=%fused_computation.15 | convolution fusion | flops 528629760 | bytes 4481024 | tf_op jit(solution)/shard_map/dot_general | solution.py:97
  137.7 1.1 fusion.9
  139.7 1.2 multiply_reduce_fusion
  140.9 1.2 convolution_convert_fusion
  142.1 2.4 fusion.1
  146.7 85.3 %reduce-scatter.2.cloned.1.call-done = bf16[80,1792]{1,0:T(8,128)(2,1)} async-done(((bf16[1280,1792]{1,0:T(8,128)(2,1)}), bf16[80,1792]{1,0:T(8,128)(2,1)}) %reduce-scatter.2.cloned.1.call-update) | async-done | bytes 286736 | tf_op jit(solution)/shard_map/reduce_scatter | solution.py:193
  232.0 1.3 slice_bitcast_fusion.16
  233.4 1.6 slice_bitcast_fusion
  (78 shorter events, 19.9 us)
Async XLA Ops:
  7.2 12.2 %copy-start = (bf16[1792,1,144]{0,2,1:T(8,128)(2,1)S(1)}, bf16[1792,1,144]{0,2,1:T(8,128)(2,1)}, u32[]{:S(2)}) copy-start(bf16[1792,1,144]{0,2,1:T(8,128)(2,1)} %param.20) | copy-start | bytes 1548292
  7.2 28.9 %copy-start.5 = (bf16[1,2,1792]{2,1,0:T(2,128)(2,1)S(1)}, bf16[1,2,1792]{2,1,0:T(2,128)(2,1)}, u32[]{:S(2)}) copy-start(bf16[1,2,1792]{2,1,0:T(2,128)(2,1)} %param.15) | copy-start | bytes 21508
  9.4 26.6 %collective-permute-start = (bf16[2,1792]{1,0:T(2,128)(2,1)S(1)}, bf16[2,1792]{1,0:T(2,128)(2,1)S(1)}, u32[]{:S(2)}, u32[]{:S(2)}) collective-permute-start(bf16[2,1792]{1,0:T(2,128)(2,1)S(1)} %slice.116), channel_id=1, source_target_pairs={{0,32},{32,64},{64,96},{96,128},{128,160},{160,192},{192,224},{224... | collective-permute-start | bytes 21512 | tf_op jit(solution)/shard_map/ppermute | solution.py:26
  20.5 28.5 %all-to-all-start.1 = ((bf16[32,2,145]{2,1,0:T(2,128)(2,1)}), bf16[32,2,145]{2,1,0:T(2,128)(2,1)S(1)}, u32[]{:S(2)}, u32[]{:S(2)}) async-start(bf16[32,2,145]{2,1,0:T(2,128)(2,1)} %pad_maximum_fusion), calls=%async_computation.1 | async-start | bytes 65536 | tf_op jit(solution)/shard_map/all_to_all | solution.py:167
  37.0 13.3 %copy-start.1 = (f32[1,16,1,112,273]{3,2,4,1,0:T(1,128)S(1)}, f32[1,16,1,112,273]{3,2,4,1,0:T(1,128)}, u32[]{:S(2)}) copy-start(f32[1,16,1,112,273]{3,2,4,1,0:T(1,128)} %param.23) | copy-start | bytes 5870596
  42.7 10.4 %copy-start.6 = (f32[112]{0:T(128)S(1)}, f32[112]{0:T(128)}, u32[]{:S(2)}) copy-start(f32[112]{0:T(128)} %param.21) | copy-start | bytes 1348
  53.8 22.5 %all-to-all-start.2 = ((bf16[32,2,112]{2,1,0:T(2,128)(2,1)}), bf16[32,2,112]{2,1,0:T(2,128)(2,1)S(1)}, u32[]{:S(2)}, u32[]{:S(2)}) async-start(bf16[32,2,112]{2,1,0:T(2,128)(2,1)} %bitcast.41), calls=%async_computation.2 | async-start | bytes 32768 | tf_op jit(solution)/shard_map/all_to_all | solution.py:179
  76.3 8.8 %copy-start.2 = (bf16[112,1792]{1,0:T(8,128)(2,1)S(1)}, bf16[112,1792]{1,0:T(8,128)(2,1)}, u32[]{:S(2)}) copy-start(bf16[112,1792]{1,0:T(8,128)(2,1)} %param.22) | copy-start | bytes 1204228
  76.3 58.0 %all-to-all-start = ((bf16[16,64,1792]{2,1,0:T(8,128)(2,1)}), bf16[16,64,1792]{2,1,0:T(8,128)(2,1)}, u32[]{:S(2)}, u32[]{:S(2)}) async-start(bf16[16,64,1792]{2,1,0:T(8,128)(2,1)} %bitcast.5), calls=%async_computation | async-start | bytes 7340032 | tf_op jit(solution)/shard_map/all_to_all | solution.py:17
  83.6 148.5 %reduce-scatter.2.cloned.1.call-start = ((), (), s32[]{:S(2)}) async-start(), calls=%async_computation.4 | async-start | bytes 4874240 | tf_op jit(solution)/shard_map/reduce_scatter | solution.py:193
  137.7 2.0 copy-start.3
  144.5 1.0 copy-start.4
Sparse Core Ops, SparseCore 0:
  144.7 87.3 reduce-scatter.1
